TPU v7x, 256 devices: a whole 4x4x8 slice. The times are simulated.
256 devices in a mesh: leaf: 64 (over z, y, core), off: 4 (over x).
Axes of the slice: x: 4, y: 4, z: 8, core: 2. Of those that a mesh axis runs over, the one named last changes fastest.
Arguments:
- multipoles: bfloat16 [65536, 488], P('leaf'), may hold values from -6 to 6
- kernels: bfloat16 [40, 488, 488], P('off'), may hold values from -0.0390625 to 0.0390625
- transfer: bfloat16 [8, 488, 488], replicated, may hold values from -0.09375 to 0.09375
- leaf_target: int32 [64, 40, 1024], P('leaf', 'off'), may hold values from 0 to 1023, as said below
- leaf_source: int32 [64, 40, 1024], P('leaf', 'off'), may hold values from 0 to 1407
- leaf_count: int32 [64, 40], P('leaf', 'off'), may hold values from 512 to 1024
- coarse_target: int32 [64, 40, 128], P('leaf', 'off'), may hold values from 0 to 127, as said below
- coarse_source: int32 [64, 40, 128], P('leaf', 'off'), may hold values from 0 to 223
- coarse_count: int32 [64, 40], P('leaf', 'off'), may hold values from 64 to 128
- ghost_send: int32 [64, 6, 64], P('leaf'), may hold values from 0 to 1343, as said below
- coarse_send: int32 [64, 6, 16], P('leaf'), may hold values from 0 to 207, as said below
Outputs:
- expansions: float32 [65536, 488], P(('leaf', 'off'))
Inputs may be any that keep to these rules, and one draw needn't show every extreme that they name: Per partition and class, leaf_target is a permutation of 0 to 1023. Per partition and class, coarse_target is a permutation of 0 to 127. `ghost_send`: in round b every index is below 1024 + b * 64. `coarse_send`: in round b every index is below 128 + b * 16.
All inputs are finite; a program needn't handle non-finite values.
Results may differ from a plain program's by a relative error of at most 0.0009.
Values may be sent and summed in bfloat16 or wider, within the bound.
A program may use at most 64 MiB of HBM per device.

v0:
```python
import jax
import jax.numpy as jnp
from jax import lax
from jax.sharding import PartitionSpec as P


def partner(block, axis, apart):
    count = lax.axis_size(axis)
    route = []
    for low in range(count):
        high = low | 1 << apart
        if high != low and high < count:
            route += [(low, high), (high, low)]
    return lax.ppermute(block, axis, route)


def slot_tables(target, source, pair_count):
    inverse = jnp.argsort(target, axis=-1)
    source_ids = jnp.take_along_axis(source, inverse, axis=-1)
    usable = inverse < pair_count[:, None]
    return (source_ids, usable)


def class_sum(buffer, source_ids, usable, kernels, num_rows):
    width = buffer.shape[1]

    def add_class(class_index, running):
        chosen = buffer[source_ids[class_index]]
        chosen = jnp.where(usable[class_index][:, None], chosen, jnp.zeros((), chosen.dtype))
        return running + jnp.dot(chosen, kernels[class_index], preferred_element_type=jnp.float32)

    return lax.fori_loop(0, kernels.shape[0], add_class, jnp.zeros((num_rows, width), jnp.float32))


def spread_down(coarse_local, transfer):
    coarse_high = coarse_local.astype(jnp.bfloat16)
    coarse_low = (coarse_local - coarse_high.astype(jnp.float32)).astype(jnp.bfloat16)
    high_part = jnp.einsum("jq,opq->jop", coarse_high, transfer, preferred_element_type=jnp.float32)
    low_part = jnp.einsum("jq,opq->jop", coarse_low, transfer, preferred_element_type=jnp.float32)
    return (high_part + low_part).reshape(-1, transfer.shape[1])


def on_device(
    multipoles,
    kernels,
    transfer,
    leaf_target,
    leaf_source,
    leaf_count,
    coarse_target,
    coarse_source,
    coarse_count,
    ghost_send,
    coarse_send,
):
    width = multipoles.shape[1]
    rounds = lax.axis_size("leaf").bit_length() - 1
    parent = jnp.dot(
        multipoles.reshape(-1, 8 * width),
        transfer.reshape(8 * width, width),
        preferred_element_type=jnp.float32,
    ).astype(jnp.bfloat16)
    buffer = multipoles
    coarse_buffer = parent
    for bit_index in range(rounds):
        arrived = partner(buffer[ghost_send[0, bit_index]], "leaf", bit_index)
        buffer = jnp.concatenate([buffer, arrived], axis=0)
    for bit_index in range(rounds):
        arrived = partner(coarse_buffer[coarse_send[0, bit_index]], "leaf", bit_index)
        coarse_buffer = jnp.concatenate([coarse_buffer, arrived], axis=0)
    leaf_ids, leaf_usable = slot_tables(leaf_target[0], leaf_source[0], leaf_count[0])
    coarse_ids, coarse_usable = slot_tables(coarse_target[0], coarse_source[0], coarse_count[0])
    parent_rows = coarse_ids.shape[1]
    coarse_local = 0.5 * class_sum(coarse_buffer, coarse_ids, coarse_usable, kernels, parent_rows)
    box_rows = multipoles.shape[0]
    row_count = box_rows // lax.axis_size("off")
    partial_sum = class_sum(buffer, leaf_ids, leaf_usable, kernels, box_rows) + spread_down(
        coarse_local, transfer
    )
    total = lax.psum(partial_sum, "off")
    return lax.dynamic_slice_in_dim(total, lax.axis_index("off") * row_count, row_count, 0)


def solution(mesh):
    in_specs = (
        P("leaf", None),
        P("off", None, None),
        P(),
        P("leaf", "off", None),
        P("leaf", "off", None),
        P("leaf", "off"),
        P("leaf", "off", None),
        P("leaf", "off", None),
        P("leaf", "off"),
        P("leaf", None, None),
        P("leaf", None, None),
    )
    out_specs = P(("leaf", "off"), None)
    return jax.shard_map(
        on_device, mesh=mesh, in_specs=in_specs, out_specs=out_specs, check_vma=False
    )
```

profile of v0, /device:TPU:16, one launch (start us, length us, event | category | flops | bytes accessed | tf_op | source)
XLA Modules:
  0.0 464.4 jit_solution(14745265589959208753)
XLA Ops:
  12.5 3.8 convolution_convert_fusion
  25.2 7.9 %gather_fusion.15 = s32[1280]{0:T(1024)S(1)} fusion(s32[10,128]{1,0:T(8,128)S(1)} %bitcast.121, s32[1280]{0:T(1024)S(1)} %fusion.23), kind=kCustom, calls=%fused_computation.15 | custom fusion | bytes 20480 | tf_op jit(solution)/shard_map/jit(take_along_axis)/gather | solution.py:19
  36.9 4.0 collective-permute-done.7
  43.5 2.2 collective-permute-start.8
  47.0 3.1 collective-permute-done.8
  58.0 2.8 gather_fusion.3
  67.2 3.3 collective-permute-start.10
  73.4 124.8 %gather_fusion.14 = s32[10240]{0:T(1024)} fusion(s32[10,1024]{1,0:T(8,128)S(1)} %bitcast.120, s32[10240]{0:T(1024)S(1)} %reshape.544), kind=kCustom, calls=%fused_computation.14 | custom fusion | bytes 163840 | tf_op jit(solution)/shard_map/jit(take_along_axis)/gather | solution.py:19
  207.4 4.5 collective-permute-start.11
  212.5 4.3 collective-permute-done.11
  216.9 2.8 concatenate.57
  220.7 29.9 %while.29 = (s32[]{:T(128)}, f32[128,488]{0,1:T(8,128)S(1)}, pred[10,128]{1,0:T(8,128)(4,1)}, s32[10,128]{1,0:T(8,128)S(1)}, bf16[224,488]{1,0:T(8,128)(2,1)S(1)...) while((s32[]{:T(128)}, f32[128,488]{0,1:T(8,128)S(1)}, pred[10,128]{1,0:T(8,128)(4,1)}, ...), condition=%wide.region_5.6_spmd.clone, body=%wide.region_4.5_spmd.clone.sunk | while | flops 61153664 | bytes 1380851 | solution.py:32
  250.6 2.0 pad_maximum_fusion.1
  252.7 2.3 gather_fusion.4
  257.2 3.6 collective-permute-done.2
  260.8 2.0 pad_maximum_fusion
  262.8 2.3 gather_fusion.5
  266.5 3.0 collective-permute-done.3
  270.2 2.3 gather_fusion.6
  273.1 4.6 fusion.17
  279.1 2.3 gather_fusion.7
  281.4 6.0 %collective-permute-start.5 = (bf16[64,488]{1,0:T(8,128)(2,1)S(1)}, bf16[64,488]{1,0:T(8,128)(2,1)S(1)}, u32[]{:S(2)}, u32[]{:S(2)}) collective-permute-start(bf16[64,488]{1,0:T(8,128)(2,1)S(1)} %gather_fusion.7), channel_id=1, source_target_pairs={{0,128},{128,0},{4,132},{132,4},{8,136},{136,8},{12,140},{140,12},... | collective-permute-start | bytes 187400 | tf_op jit(solution)/shard_map/ppermute | solution.py:14
  287.4 5.3 %convolution_add_fusion.1 = f32[128,8,488]{0,2,1:T(8,128)} fusion(f32[128,8,488]{0,2,1:T(8,128)} %fusion.17, bf16[8,488,488]{2,1,0:T(8,128)(2,1)} %param.17, f32[128,488]{0,1:T(8,128)S(1)} %get-tuple-element.228), kind=kOutput, calls=%fused_computation.42 | convolution fusion | flops 488530944 | bytes 8057856 | tf_op jit(solution)/shard_map/jq,opq->jop/dot_general | solution.py:39
  292.7 3.1 copy.53
  295.8 93.2 %while.28 = (s32[]{:T(128)}, f32[1024,488]{0,1:T(8,128)}, pred[10,1024]{1,0:T(8,128)(4,1)}, s32[10,1024]{1,0:T(8,128)}, bf16[1408,488]{1,0:T(8,128)(2,1)S(1)}, /...) while((s32[]{:T(128)}, f32[1024,488]{0,1:T(8,128)}, pred[10,1024]{1,0:T(8,128)(4,1)}, ...), condition=%wide.region_2.3_spmd.clone, body=%wide.region_1.2_spmd.clone.sunk | while | flops 489222144 | bytes 7519347 | solution.py:32
  296.6 4.0 gather_fusion
  301.3 3.2 select_add_fusion.2
  305.3 4.0 gather_fusion
  310.0 3.9 select_add_fusion.2
  314.7 4.0 gather_fusion
  319.4 3.9 select_add_fusion.2
  324.1 4.0 gather_fusion
  328.8 3.9 select_add_fusion.2
  333.5 4.0 gather_fusion
  338.2 3.9 select_add_fusion.2
  342.8 4.0 gather_fusion
  347.5 3.9 select_add_fusion.2
  352.2 4.0 gather_fusion
  356.9 3.9 select_add_fusion.2
  361.6 4.0 gather_fusion
  366.3 3.9 select_add_fusion.2
  371.0 4.0 gather_fusion
  375.7 3.9 select_add_fusion.2
  380.4 4.0 gather_fusion
  385.1 3.9 select_add_fusion.2
  389.0 3.0 copy.54
  392.0 3.2 bitcast_add_fusion
  395.2 60.6 %all-reduce.2.cloned.1.call-done = f32[1024,488]{1,0:T(8,128)} async-done(((f32[1024,488]{1,0:T(8,128)}), f32[1024,488]{1,0:T(8,128)}) %all-reduce.2.cloned.1.call-update) | async-done | bytes 1998864 | tf_op jit(solution)/shard_map/psum | solution.py:80
  (189 shorter events, 103.2 us)
Async XLA Ops:
  6.5 1.5 copy-start.7
  6.5 1.6 copy-start.8
  6.5 2.9 copy-start.5
  6.5 17.9 %sort.39.cloned.1.call-start = ((), (), s32[]{:S(2)}) async-start(), calls=%async_computation.2 | async-start | bytes 49184 | tf_op jit(solution)/shard_map/jit(argsort)/sort | solution.py:18
  9.5 47.4 %collective-permute-start = (bf16[64,488]{1,0:T(8,128)(2,1)}, bf16[64,488]{1,0:T(8,128)(2,1)S(1)}, u32[]{:S(2)}, u32[]{:S(2)}) collective-permute-start(bf16[64,488]{1,0:T(8,128)(2,1)} %gather_fusion.2), channel_id=1, source_target_pairs={{0,4},{4,0},{8,12},{12,8},{16,20},{20,16},{24,28},{28,24},{32,36},... | collective-permute-start | bytes 187400 | tf_op jit(solution)/shard_map/ppermute | solution.py:14
  10.7 60.4 %sort.37.cloned.1.call-start = ((), (), s32[]{:S(2)}) async-start(), calls=%async_computation.1 | async-start | bytes 393248 | tf_op jit(solution)/shard_map/jit(argsort)/sort | solution.py:18
  12.5 5.4 %copy-start.3 = (s32[1,10,1024]{2,0,1:T(1,128)S(1)}, s32[1,10,1024]{2,0,1:T(1,128)}, u32[]{:S(2)}) copy-start(s32[1,10,1024]{2,0,1:T(1,128)} %param.18) | copy-start | bytes 122884
  17.3 15.8 %collective-permute-start.6 = (bf16[16,488]{0,1:T(8,128)(2,1)S(1)}, bf16[16,488]{0,1:T(8,128)(2,1)S(1)}, u32[]{:S(2)}, u32[]{:S(2)}) collective-permute-start(bf16[16,488]{0,1:T(8,128)(2,1)S(1)} %copy.41), channel_id=1, source_target_pairs={{0,4},{4,0},{8,12},{12,8},{16,20},{20,16},{24,28},{28,24},{32,36},... | collective-permute-start | bytes 46856 | tf_op jit(solution)/shard_map/ppermute | solution.py:14
  19.2 436.6 %all-reduce.2.cloned.1.call-start = ((), (), s32[]{:S(2)}) async-start(), calls=%async_computation | async-start | bytes 4194304 | tf_op jit(solution)/shard_map/psum | solution.py:80
  19.3 1.6 copy-start.4
  19.3 4.5 copy-start.6
  25.2 11.8 %copy-start.2 = (s32[10,128]{1,0:T(8,128)S(1)}, s32[10,128]{1,0:T(8,128)}, u32[]{:S(2)}) copy-start(s32[10,128]{1,0:T(8,128)} %get-tuple-element.227) | copy-start | bytes 15364
  35.6 5.4 %collective-permute-start.7 = (bf16[16,488]{0,1:T(8,128)(2,1)S(1)}, bf16[16,488]{0,1:T(8,128)(2,1)S(1)}, u32[]{:S(2)}, u32[]{:S(2)}) collective-permute-start(bf16[16,488]{0,1:T(8,128)(2,1)S(1)} %copy.43), channel_id=1, source_target_pairs={{0,8},{8,0},{4,12},{12,4},{16,24},{24,16},{20,28},{28,20},{32,40},... | collective-permute-start | bytes 46856 | tf_op jit(solution)/shard_map/ppermute | solution.py:14
  43.5 6.5 %collective-permute-start.8 = (bf16[16,488]{0,1:T(8,128)(2,1)S(1)}, bf16[16,488]{0,1:T(8,128)(2,1)S(1)}, u32[]{:S(2)}, u32[]{:S(2)}) collective-permute-start(bf16[16,488]{0,1:T(8,128)(2,1)S(1)} %copy.45), channel_id=1, source_target_pairs={{0,16},{16,0},{4,20},{20,4},{8,24},{24,8},{12,28},{28,12},{32,48},... | collective-permute-start | bytes 46856 | tf_op jit(solution)/shard_map/ppermute | solution.py:14
  54.9 7.2 %collective-permute-start.9 = (bf16[16,488]{0,1:T(8,128)(2,1)}, bf16[16,488]{0,1:T(8,128)(2,1)S(1)}, u32[]{:S(2)}, u32[]{:S(2)}) collective-permute-start(bf16[16,488]{0,1:T(8,128)(2,1)} %copy.47), channel_id=1, source_target_pairs={{0,32},{32,0},{4,36},{36,4},{8,40},{40,8},{12,44},{44,12},{16,48},... | collective-permute-start | bytes 46856 | tf_op jit(solution)/shard_map/ppermute | solution.py:14
  60.8 189.8 %collective-permute-start.1 = (bf16[64,488]{1,0:T(8,128)(2,1)}, bf16[64,488]{1,0:T(8,128)(2,1)}, u32[]{:S(2)}, u32[]{:S(2)}) collective-permute-start(bf16[64,488]{1,0:T(8,128)(2,1)} %gather_fusion.3), channel_id=1, source_target_pairs={{0,8},{8,0},{4,12},{12,4},{16,24},{24,16},{20,28},{28,20},{32,40},... | collective-permute-start | bytes 187400 | tf_op jit(solution)/shard_map/ppermute | solution.py:14
  67.2 134.1 %collective-permute-start.10 = (bf16[16,488]{0,1:T(8,128)(2,1)}, bf16[16,488]{0,1:T(8,128)(2,1)}, u32[]{:S(2)}, u32[]{:S(2)}) collective-permute-start(bf16[16,488]{0,1:T(8,128)(2,1)} %copy.49), channel_id=1, source_target_pairs={{0,64},{64,0},{4,68},{68,4},{8,72},{72,8},{12,76},{76,12},{16,80},... | collective-permute-start | bytes 46856 | tf_op jit(solution)/shard_map/ppermute | solution.py:14
  198.3 13.6 %copy-start.1 = (s32[10,1024]{1,0:T(8,128)S(1)}, s32[10,1024]{1,0:T(8,128)}, u32[]{:S(2)}) copy-start(s32[10,1024]{1,0:T(8,128)} %get-tuple-element.225) | copy-start | bytes 122884
  198.3 13.6 %copy-start.9 = (s32[1,10]{1,0:T(1,128)S(1)}, s32[1,10]{1,0:T(1,128)}, u32[]{:S(2)}) copy-start(s32[1,10]{1,0:T(1,128)} %param.20) | copy-start | bytes 124
  207.4 9.5 %collective-permute-start.11 = (bf16[16,488]{0,1:T(8,128)(2,1)}, bf16[16,488]{0,1:T(8,128)(2,1)}, u32[]{:S(2)}, u32[]{:S(2)}) collective-permute-start(bf16[16,488]{0,1:T(8,128)(2,1)} %copy.51), channel_id=1, source_target_pairs={{0,128},{128,0},{4,132},{132,4},{8,136},{136,8},{12,140},{140,12},... | collective-permute-start | bytes 46856 | tf_op jit(solution)/shard_map/ppermute | solution.py:14
  254.9 5.9 %collective-permute-start.2 = (bf16[64,488]{1,0:T(8,128)(2,1)S(1)}, bf16[64,488]{1,0:T(8,128)(2,1)S(1)}, u32[]{:S(2)}, u32[]{:S(2)}) collective-permute-start(bf16[64,488]{1,0:T(8,128)(2,1)S(1)} %gather_fusion.4), channel_id=1, source_target_pairs={{0,16},{16,0},{4,20},{20,4},{8,24},{24,8},{12,28},{28,12},{32,48},... | collective-permute-start | bytes 187400 | tf_op jit(solution)/shard_map/ppermute | solution.py:14
  265.1 4.4 collective-permute-start.3
  272.5 6.0 %collective-permute-start.4 = (bf16[64,488]{1,0:T(8,128)(2,1)S(1)}, bf16[64,488]{1,0:T(8,128)(2,1)S(1)}, u32[]{:S(2)}, u32[]{:S(2)}) collective-permute-start(bf16[64,488]{1,0:T(8,128)(2,1)S(1)} %gather_fusion.6), channel_id=1, source_target_pairs={{0,64},{64,0},{4,68},{68,4},{8,72},{72,8},{12,76},{76,12},{16,80},... | collective-permute-start | bytes 187400 | tf_op jit(solution)/shard_map/ppermute | solution.py:14
  281.4 14.4 %collective-permute-start.5 = (bf16[64,488]{1,0:T(8,128)(2,1)S(1)}, bf16[64,488]{1,0:T(8,128)(2,1)S(1)}, u32[]{:S(2)}, u32[]{:S(2)}) collective-permute-start(bf16[64,488]{1,0:T(8,128)(2,1)S(1)} %gather_fusion.7), channel_id=1, source_target_pairs={{0,128},{128,0},{4,132},{132,4},{8,136},{136,8},{12,140},{140,12},... | collective-permute-start | bytes 187400 | tf_op jit(solution)/shard_map/ppermute | solution.py:14
  389.0 3.0 copy-start
Sparse Core Ops, SparseCore 0:
  10.8 2.2 sort.43.cloned.1.call-done
  19.3 4.6 sort.41.cloned.1.call-done
  395.3 60.4 all-reduce.1
  (2 shorter events, 0.0 us)
where the time goes:
time: 469 us; the launch traced here: 464 us
  local copies, waits for them, and re-layouts  255 us (54%)
  waiting for transfers between devices  79.4 us (17%)
  matrix products  66.4 us (14%)
  other arithmetic  26.5 us (6%)
  starting transfers between devices  23.1 us (5%)
  between operations  13.4 us (3%)
    gather x4, local copies, waits for them, and re-layouts, slot_tables(): source_ids = jnp.take_along_axis(source, inverse, axis=-1)  135 us
    psum x1, waiting for transfers between devices, on_device(): total = lax.psum(partial_sum, 'off')  60.6 us
    dot_general x20, matrix products, add_class(): jnp.dot(chosen, kernels[class_index], preferred_element_type=jnp.float32)  52.7 us
    gather x20, local copies, waits for them, and re-layouts, add_class(): chosen = buffer[source_ids[class_index]]  48.1 us
    ppermute x12, starting transfers between devices, partner(): return lax.ppermute(block, axis, route)  23.1 us
    ppermute x12, waiting for transfers between devices, partner(): return lax.ppermute(block, axis, route)  18.8 us
    gather x6, local copies, waits for them, and re-layouts, on_device(): arrived = partner(buffer[ghost_send[0, bit_index]], 'leaf', bit_index)  13.4 us
    concatenate x8, local copies, waits for them, and re-layouts, on_device(): coarse_buffer = jnp.concatenate([coarse_buffer, arrived], axis=0)  12.4 us
  transfers between devices with their start and end apart: 13, of which 7 were waited for; matrix products, arithmetic and copies ran while one was open for 49% of the time, Pallas kernels for 0%

commit v1 on v0

v1 whole, which is shorter than its diff:
```python
import jax
import jax.numpy as jnp
from jax import lax
from jax.sharding import PartitionSpec as P


def partner(block, axis, apart):
    count = lax.axis_size(axis)
    route = []
    for low in range(count):
        high = low | 1 << apart
        if high != low and high < count:
            route += [(low, high), (high, low)]
    return lax.ppermute(block, axis, route)


def slot_table(target, source, pair_count, pad_row):
    pair = lax.broadcasted_iota(jnp.int32, target.shape, 1)
    payload = jnp.where(pair < pair_count[:, None], source, pad_row)
    _, slot = lax.sort((target, payload), dimension=1, num_keys=1)
    return slot


def class_sum(buffer, slot, kernels):
    width = buffer.shape[1]
    aligned = buffer.at[slot.T].get(mode="fill", fill_value=0)
    flat = aligned.reshape(aligned.shape[0], -1)
    return jnp.dot(flat, kernels.reshape(-1, width), preferred_element_type=jnp.float32)


def spread_down(coarse_local, transfer):
    coarse_high = coarse_local.astype(jnp.bfloat16)
    coarse_low = (coarse_local - coarse_high.astype(jnp.float32)).astype(jnp.bfloat16)
    high_part = jnp.einsum("jq,opq->jop", coarse_high, transfer, preferred_element_type=jnp.float32)
    low_part = jnp.einsum("jq,opq->jop", coarse_low, transfer, preferred_element_type=jnp.float32)
    return (high_part + low_part).reshape(-1, transfer.shape[1])


def exchange(owned, send, rows_per_round, rounds):
    width = owned.shape[1]
    total = owned.shape[0] + rounds * rows_per_round
    buffer = jnp.zeros((total, width), owned.dtype)
    buffer = lax.dynamic_update_slice(buffer, owned, (0, 0))
    for bit_index in range(rounds):
        arrived = partner(buffer[send[0, bit_index]], "leaf", bit_index)
        at = owned.shape[0] + bit_index * rows_per_round
        buffer = lax.dynamic_update_slice(buffer, arrived, (at, 0))
    return buffer


def on_device(
    multipoles,
    kernels,
    transfer,
    leaf_target,
    leaf_source,
    leaf_count,
    coarse_target,
    coarse_source,
    coarse_count,
    ghost_send,
    coarse_send,
):
    width = multipoles.shape[1]
    rounds = lax.axis_size("leaf").bit_length() - 1
    parent = jnp.dot(
        multipoles.reshape(-1, 8 * width),
        transfer.reshape(8 * width, width),
        preferred_element_type=jnp.float32,
    ).astype(jnp.bfloat16)
    buffer = exchange(multipoles, ghost_send, ghost_send.shape[2], rounds)
    coarse_buffer = exchange(parent, coarse_send, coarse_send.shape[2], rounds)
    leaf_slot = slot_table(leaf_target[0], leaf_source[0], leaf_count[0], buffer.shape[0])
    coarse_slot = slot_table(coarse_target[0], coarse_source[0], coarse_count[0], coarse_buffer.shape[0])
    coarse_local = 0.5 * class_sum(coarse_buffer, coarse_slot, kernels)
    partial_sum = class_sum(buffer, leaf_slot, kernels) + spread_down(coarse_local, transfer)
    return lax.psum_scatter(partial_sum, "off", scatter_dimension=0, tiled=True)


def solution(mesh):
    in_specs = (
        P("leaf", None),
        P("off", None, None),
        P(),
        P("leaf", "off", None),
        P("leaf", "off", None),
        P("leaf", "off"),
        P("leaf", "off", None),
        P("leaf", "off", None),
        P("leaf", "off"),
        P("leaf", None, None),
        P("leaf", None, None),
    )
    out_specs = P(("leaf", "off"), None)
    return jax.shard_map(
        on_device, mesh=mesh, in_specs=in_specs, out_specs=out_specs, check_vma=False
    )
```

time: 469 us -> 247 us (0.53)
  local copies, waits for them, and re-layouts: 255 us -> 101 us
  waiting for transfers between devices: 79.4 us -> 42.6 us
  matrix products: 66.4 us -> 34.1 us
  starting transfers between devices: 23.1 us -> 28.5 us
    gather x42 -> x22, local copies, waits for them, and re-layouts: 208 us -> 83.5 us  [the longest x4 72 us: class_sum(): aligned = buffer.at[slot.T].get(mode='fill', fill_value=0)]
    psum x1 -> x0, waiting for transfers between devices: 60.6 us -> none  [on_device(): total = lax.psum(partial_sum, 'off')]
    dot_general x20 -> x2, matrix products: 52.7 us -> 21.9 us  [class_sum(): jnp.dot(flat, kernels.reshape(-1, width), preferred_element_type=jnp.floa...]
    reduce_scatter x0 -> x1, waiting for transfers between devices: none -> 29.1 us  [on_device(): return lax.psum_scatter(partial_sum, 'off', scatter_dimension=0, tiled=True)]
    concatenate x10 -> x0, local copies, waits for them, and re-layouts: 13.1 us -> none  [the longest x8 12.4 us: on_device(): coarse_buffer = jnp.concatenate([coarse_buffer, arrived], axis=0)]
    select_n x24 -> x8, other arithmetic: 9.32 us -> 20.9 us  [the longest x4 18.7 us: class_sum(): aligned = buffer.at[slot.T].get(mode='fill', fill_value=0)]
    dynamic_slice x12 -> x0, local copies, waits for them, and re-layouts: 9.32 us -> none  [the longest x10 7.26 us: add_class(): usable[class_index][:, None]]
    dynamic_update_slice x0 -> x21, local copies, waits for them, and re-layouts: none -> 7.11 us  [the longest x18 6.8 us: exchange(): buffer = lax.dynamic_update_slice(buffer, arrived, (at, 0))]
  transfers between devices with their start and end apart: 13 -> 13, of which waited for: 7 -> 6; matrix products, arithmetic and copies ran while one was open for 49% -> 21% of each run, Pallas kernels for 0% -> 0%
where the time goes in v1:
time: 247 us; the launch traced here: 244 us
  local copies, waits for them, and re-layouts  101 us (41%)
  waiting for transfers between devices  42.6 us (17%)
  matrix products  34.1 us (14%)
  starting transfers between devices  28.5 us (12%)
  other arithmetic  24 us (10%)
  between operations  13.5 us (5%)
    gather x4, local copies, waits for them, and re-layouts, class_sum(): aligned = buffer.at[slot.T].get(mode='fill', fill_value=0)  72 us
    reduce_scatter x1, waiting for transfers between devices, on_device(): return lax.psum_scatter(partial_sum, 'off', scatter_dimension=0, tiled=True)  29.1 us
    ppermute x12, starting transfers between devices, partner(): return lax.ppermute(block, axis, route)  28.4 us
    dot_general x2, matrix products, class_sum(): jnp.dot(flat, kernels.reshape(-1, width), preferred_element_type=jnp.floa...  21.9 us
    select_n x4, other arithmetic, class_sum(): aligned = buffer.at[slot.T].get(mode='fill', fill_value=0)  18.7 us
    ppermute x12, waiting for transfers between devices, partner(): return lax.ppermute(block, axis, route)  13.5 us
    gather x18, local copies, waits for them, and re-layouts, exchange(): arrived = partner(buffer[send[0, bit_index]], 'leaf', bit_index)  11.5 us
    dynamic_update_slice x18, local copies, waits for them, and re-layouts, exchange(): buffer = lax.dynamic_update_slice(buffer, arrived, (at, 0))  6.8 us
  transfers between devices with their start and end apart: 13, of which 6 were waited for; matrix products, arithmetic and copies ran while one was open for 21% of the time, Pallas kernels for 0%

profile of v1, /device:TPU:16, one launch (start us, length us, event | category | flops | bytes accessed | tf_op | source)
XLA Modules:
  0.0 244.0 jit_solution(7195277285148868595)
XLA Ops:
  6.5 0.7 fusion.23
  7.3 1.5 copy.53
  8.9 1.3 gather_fusion
  10.3 1.8 reshape.361
  12.2 3.9 %convolution_convert_fusion = bf16[128,488]{0,1:T(8,128)(2,1)S(1)} fusion(bf16[128,3904]{1,0:T(8,128)(2,1)S(1)} %reshape.361, bf16[3904,488]{1,0:T(8,128)(2,1)} %bitcast.88), kind=kOutput, calls=%fused_computation.24 | convolution fusion | flops 487781376 | bytes 4934656 | tf_op jit(solution)/shard_map/dot_general | solution.py:66
  18.9 0.7 bitcast_select_fusion
  22.2 0.7 compare_select_fusion.1
  24.2 1.4 collective-permute-start.7
  25.6 0.7 compare_and_fusion.1
  26.5 3.1 %collective-permute-done.7 = bf16[16,488]{0,1:T(8,128)(2,1)S(1)} collective-permute-done((bf16[16,488]{0,1:T(8,128)(2,1)S(1)}, bf16[16,488]{0,1:T(8,128)(2,1)S(1)}, u32[]{:S(2)}, u32[]{:S(2)}) %collective-permute-start.7) | collective-permute-done | bytes 15648 | tf_op jit(solution)/shard_map/ppermute | solution.py:14
  29.6 0.8 dynamic_update_slice.51
  31.2 2.2 collective-permute-start.8
  33.5 4.2 %collective-permute-done.8 = bf16[16,488]{0,1:T(8,128)(2,1)S(1)} collective-permute-done((bf16[16,488]{0,1:T(8,128)(2,1)S(1)}, bf16[16,488]{0,1:T(8,128)(2,1)S(1)}, u32[]{:S(2)}, u32[]{:S(2)}) %collective-permute-start.8) | collective-permute-done | bytes 15648 | tf_op jit(solution)/shard_map/ppermute | solution.py:14
  37.7 0.8 dynamic_update_slice.52
  39.4 2.0 collective-permute-start.9
  41.4 0.8 constant_dynamic-update-slice_fusion.5
  42.3 0.7 gather_fusion.1
  43.0 1.6 collective-permute-start.1
  44.5 0.8 dynamic_update_slice.53
  46.2 3.4 %collective-permute-start.10 = (bf16[16,488]{0,1:T(8,128)(2,1)S(1)}, bf16[16,488]{0,1:T(8,128)(2,1)S(1)}, u32[]{:S(2)}, u32[]{:S(2)}) collective-permute-start(bf16[16,488]{0,1:T(8,128)(2,1)S(1)} %copy.68), channel_id=1, source_target_pairs={{0,64},{64,0},{4,68},{68,4},{8,72},{72,8},{12,76},{76,12},{16,80},... | collective-permute-start | bytes 46856 | tf_op jit(solution)/shard_map/ppermute | solution.py:14
  49.6 0.9 compare_select_fusion
  51.7 0.8 collective-permute-done.10
  52.4 0.8 dynamic_update_slice.54
  54.1 8.2 %collective-permute-start.11 = (bf16[16,488]{0,1:T(8,128)(2,1)S(1)}, bf16[16,488]{0,1:T(8,128)(2,1)S(1)}, u32[]{:S(2)}, u32[]{:S(2)}) collective-permute-start(bf16[16,488]{0,1:T(8,128)(2,1)S(1)} %copy.70), channel_id=1, source_target_pairs={{0,128},{128,0},{4,132},{132,4},{8,136},{136,8},{12,140},{140,12},... | collective-permute-start | bytes 46856 | tf_op jit(solution)/shard_map/ppermute | solution.py:14
  62.4 0.9 copy.52
  63.3 2.0 collective-permute-done.11
  65.2 0.8 dynamic_update_slice.55
  66.2 4.1 %gather_fusion.13 = bf16[1280,488]{1,0:T(8,128)(2,1)S(1)} fusion(bf16[224,488]{1,0:T(8,128)(2,1)S(1)} %copy.72, s32[2048]{0:T(1024)S(1)} %pad_clamp_fusion), kind=kCustom, calls=%fused_computation.13 | custom fusion | bytes 2503680 | tf_op jit(solution)/shard_map/gather | solution.py:26
  70.3 1.6 reshape.469
  71.9 1.3 gather_fusion.2
  73.9 1.8 broadcast_select_fusion.1
  75.7 3.5 %collective-permute-done.2 = bf16[64,488]{1,0:T(8,128)(2,1)S(1)} collective-permute-done((bf16[64,488]{1,0:T(8,128)(2,1)}, bf16[64,488]{1,0:T(8,128)(2,1)S(1)}, u32[]{:S(2)}, u32[]{:S(2)}) %collective-permute-start.2) | collective-permute-done | bytes 62496 | tf_op jit(solution)/shard_map/ppermute | solution.py:14
  79.2 1.4 gather_fusion.3
  80.8 5.7 %fusion.9 = f32[128,488]{0,1:T(8,128)} fusion(bf16[10,488,488]{2,1,0:T(8,128)(2,1)} %param.12, bf16[128,10,488]{2,1,0:T(8,128)(2,1)S(1)} %broadcast_select_fusion.1), kind=kOutput, calls=%fused_computation.23 | convolution fusion | flops 609711104 | bytes 6262016 | tf_op jit(solution)/shard_map/dot_general | solution.py:28
  86.5 0.8 gather_fusion.4
  87.4 3.5 %collective-permute-start.4 = (bf16[64,488]{1,0:T(8,128)(2,1)S(1)}, bf16[64,488]{1,0:T(8,128)(2,1)S(1)}, u32[]{:S(2)}, u32[]{:S(2)}) collective-permute-start(bf16[64,488]{1,0:T(8,128)(2,1)S(1)} %gather_fusion.4), channel_id=1, source_target_pairs={{0,64},{64,0},{4,68},{68,4},{8,72},{72,8},{12,76},{76,12},{16,80},... | collective-permute-start | bytes 187400 | tf_op jit(solution)/shard_map/ppermute | solution.py:14
  90.8 3.5 %fusion.14 = f32[128,8,488]{0,2,1:T(8,128)S(1)} fusion(bf16[8,488,488]{2,1,0:T(8,128)(2,1)} %param.13, f32[128,488]{0,1:T(8,128)} %fusion.9), kind=kOutput, calls=%fused_computation.28 | convolution fusion | flops 487781376 | bytes 6059008 | tf_op jit(solution)/shard_map/jq,opq->jop/dot_general | solution.py:34
  94.3 1.4 gather_fusion.5
  95.8 4.9 %collective-permute-start.5 = (bf16[64,488]{1,0:T(8,128)(2,1)}, bf16[64,488]{1,0:T(8,128)(2,1)}, u32[]{:S(2)}, u32[]{:S(2)}) collective-permute-start(bf16[64,488]{1,0:T(8,128)(2,1)} %gather_fusion.5), channel_id=1, source_target_pairs={{0,128},{128,0},{4,132},{132,4},{8,136},{136,8},{12,140},{140,12},... | collective-permute-start | bytes 187400 | tf_op jit(solution)/shard_map/ppermute | solution.py:14
  100.7 4.9 %convolution_add_fusion = f32[128,8,488]{0,2,1:T(8,128)} fusion(f32[128,8,488]{0,2,1:T(8,128)S(1)} %fusion.14, bf16[8,488,488]{2,1,0:T(8,128)(2,1)} %param.13, f32[128,488]{0,1:T(8,128)} %fusion.9), kind=kOutput, calls=%fused_computation.19 | convolution fusion | flops 488468480 | bytes 8057856 | tf_op jit(solution)/shard_map/jq,opq->jop/dot_general | solution.py:35
  105.6 2.2 copy.75
  107.9 1.8 copy.76
  109.7 0.8 constant_dynamic-update-slice_fusion
  110.5 45.0 %gather_fusion.6 = bf16[10240,488]{1,0:T(8,128)(2,1)} fusion(bf16[1408,488]{1,0:T(8,128)(2,1)S(1)} %constant_dynamic-update-slice_fusion, s32[10240]{0:T(1024)} %broadcast_clamp_fusion), kind=kCustom, calls=%fused_computation.6 | custom fusion | bytes 20029440 | tf_op jit(solution)/shard_map/gather | solution.py:26
  155.6 21.2 %reshape.413 = bf16[1024,10,488]{2,1,0:T(8,128)(2,1)} reshape(bf16[10240,488]{1,0:T(8,128)(2,1)} %gather_fusion.6) | data formatting | bytes 19988480 | tf_op jit(solution)/shard_map/gather | solution.py:26
  176.8 15.4 %broadcast_select_fusion = bf16[1024,10,488]{2,1,0:T(8,128)(2,1)} fusion(bf16[1024,10,488]{2,1,0:T(8,128)(2,1)} %reshape.413, pred[1024,10]{1,0:T(8,128)(4,1)S(1)} %copy-done.1), kind=kLoop, calls=%fused_computation.14 | loop fusion | flops 4997120 | bytes 19998720 | tf_op jit(solution)/shard_map/select_n | solution.py:26
  192.2 16.1 %bitcast_add_fusion = f32[1024,488]{0,1:T(8,128)} fusion(f32[1024,488]{0,1:T(8,128)S(1)} %copy-done, bf16[10,488,488]{2,1,0:T(8,128)(2,1)S(1)} %bitcast.91, bf16[1024,10,488]{2,1,0:T(8,128)(2,1)} %broadcast_select_fusion), kind=kOutput, calls=%fused_computation.18 | convolution fusion | flops 4877688832 | bytes 18754816 | tf_op jit(solution)/shard_map/dot_general | solution.py:28
  208.4 29.1 %reduce-scatter.2.cloned.1.call-done = f32[256,488]{0,1:T(8,128)} async-done(((f32[1024,488]{0,1:T(8,128)}), f32[256,488]{0,1:T(8,128)}) %reduce-scatter.2.cloned.1.call-update) | async-done | bytes 499728 | tf_op jit(solution)/shard_map/reduce_scatter | solution.py:77
  (94 shorter events, 12.9 us)
Async XLA Ops:
  6.5 15.7 %sort.35.cloned.1.call-start = ((), (), s32[]{:S(2)}) async-start(), calls=%async_computation.3 | async-start | bytes 49184 | tf_op jit(solution)/shard_map/sort | solution.py:20
  8.8 3.3 %copy-start.7 = (s32[1,6,16]{2,0,1:T(1,128)S(1)}, s32[1,6,16]{2,0,1:T(1,128)}, u32[]{:S(2)}) copy-start(s32[1,6,16]{2,0,1:T(1,128)} %param.21) | copy-start | bytes 1156
  10.3 31.1 %collective-permute-start = (bf16[64,488]{1,0:T(8,128)(2,1)}, bf16[64,488]{1,0:T(8,128)(2,1)}, u32[]{:S(2)}, u32[]{:S(2)}) collective-permute-start(bf16[64,488]{1,0:T(8,128)(2,1)} %gather_fusion), channel_id=1, source_target_pairs={{0,4},{4,0},{8,12},{12,8},{16,20},{20,16},{24,28},{28,24},{32,36},... | collective-permute-start | bytes 187400 | tf_op jit(solution)/shard_map/ppermute | solution.py:14
  12.1 5.4 %copy-start.6 = (s32[1,10,128]{2,0,1:T(1,128)S(1)}, s32[1,10,128]{2,0,1:T(1,128)}, u32[]{:S(2)}) copy-start(s32[1,10,128]{2,0,1:T(1,128)} %param.17) | copy-start | bytes 15364
  12.1 6.0 %copy-start.5 = (s32[1,10,128]{2,0,1:T(1,128)S(1)}, s32[1,10,128]{2,0,1:T(1,128)}, u32[]{:S(2)}) copy-start(s32[1,10,128]{2,0,1:T(1,128)} %param.18) | copy-start | bytes 15364
  12.1 6.0 %copy-start.9 = (s32[1,10]{1,0:T(1,128)S(1)}, s32[1,10]{1,0:T(1,128)}, u32[]{:S(2)}) copy-start(s32[1,10]{1,0:T(1,128)} %param.19) | copy-start | bytes 124
  12.2 6.8 %copy-start.3 = (s32[1,10,1024]{2,0,1:T(1,128)S(1)}, s32[1,10,1024]{2,0,1:T(1,128)}, u32[]{:S(2)}) copy-start(s32[1,10,1024]{2,0,1:T(1,128)} %param.15) | copy-start | bytes 122884
  12.2 6.8 %copy-start.8 = (s32[1,10]{1,0:T(1,128)S(1)}, s32[1,10]{1,0:T(1,128)}, u32[]{:S(2)}) copy-start(s32[1,10]{1,0:T(1,128)} %param.16) | copy-start | bytes 124
  12.2 7.4 %copy-start.4 = (s32[1,10,1024]{2,0,1:T(1,128)S(1)}, s32[1,10,1024]{2,0,1:T(1,128)}, u32[]{:S(2)}) copy-start(s32[1,10,1024]{2,0,1:T(1,128)} %param.14) | copy-start | bytes 122884
  17.0 5.9 %collective-permute-start.6 = (bf16[16,488]{0,1:T(8,128)(2,1)S(1)}, bf16[16,488]{0,1:T(8,128)(2,1)S(1)}, u32[]{:S(2)}, u32[]{:S(2)}) collective-permute-start(bf16[16,488]{0,1:T(8,128)(2,1)S(1)} %copy.60), channel_id=1, source_target_pairs={{0,4},{4,0},{8,12},{12,8},{16,20},{20,16},{24,28},{28,24},{32,36},... | collective-permute-start | bytes 46856 | tf_op jit(solution)/shard_map/ppermute | solution.py:14
  18.9 30.7 %sort.33.cloned.1.call-start = ((), (), s32[]{:S(2)}) async-start(), calls=%async_computation.2 | async-start | bytes 393248 | tf_op jit(solution)/shard_map/sort | solution.py:20
  20.3 217.2 %reduce-scatter.2.cloned.1.call-start = ((), (), s32[]{:S(2)}) async-start(), calls=%async_computation.1 | async-start | bytes 2498560 | tf_op jit(solution)/shard_map/reduce_scatter | solution.py:77
  24.2 5.4 %collective-permute-start.7 = (bf16[16,488]{0,1:T(8,128)(2,1)S(1)}, bf16[16,488]{0,1:T(8,128)(2,1)S(1)}, u32[]{:S(2)}, u32[]{:S(2)}) collective-permute-start(bf16[16,488]{0,1:T(8,128)(2,1)S(1)} %copy.62), channel_id=1, source_target_pairs={{0,8},{8,0},{4,12},{12,4},{16,24},{24,16},{20,28},{28,20},{32,40},... | collective-permute-start | bytes 46856 | tf_op jit(solution)/shard_map/ppermute | solution.py:14
  31.2 6.5 %collective-permute-start.8 = (bf16[16,488]{0,1:T(8,128)(2,1)S(1)}, bf16[16,488]{0,1:T(8,128)(2,1)S(1)}, u32[]{:S(2)}, u32[]{:S(2)}) collective-permute-start(bf16[16,488]{0,1:T(8,128)(2,1)S(1)} %copy.64), channel_id=1, source_target_pairs={{0,16},{16,0},{4,20},{20,4},{8,24},{24,8},{12,28},{28,12},{32,48},... | collective-permute-start | bytes 46856 | tf_op jit(solution)/shard_map/ppermute | solution.py:14
  39.4 5.1 %collective-permute-start.9 = (bf16[16,488]{0,1:T(8,128)(2,1)S(1)}, bf16[16,488]{0,1:T(8,128)(2,1)S(1)}, u32[]{:S(2)}, u32[]{:S(2)}) collective-permute-start(bf16[16,488]{0,1:T(8,128)(2,1)S(1)} %copy.66), channel_id=1, source_target_pairs={{0,32},{32,0},{4,36},{36,4},{8,40},{40,8},{12,44},{44,12},{16,48},... | collective-permute-start | bytes 46856 | tf_op jit(solution)/shard_map/ppermute | solution.py:14
  43.0 29.0 %collective-permute-start.1 = (bf16[64,488]{1,0:T(8,128)(2,1)S(1)}, bf16[64,488]{1,0:T(8,128)(2,1)S(1)}, u32[]{:S(2)}, u32[]{:S(2)}) collective-permute-start(bf16[64,488]{1,0:T(8,128)(2,1)S(1)} %gather_fusion.1), channel_id=1, source_target_pairs={{0,8},{8,0},{4,12},{12,4},{16,24},{24,16},{20,28},{28,20},{32,40},... | collective-permute-start | bytes 187400 | tf_op jit(solution)/shard_map/ppermute | solution.py:14
  46.2 6.2 %collective-permute-start.10 = (bf16[16,488]{0,1:T(8,128)(2,1)S(1)}, bf16[16,488]{0,1:T(8,128)(2,1)S(1)}, u32[]{:S(2)}, u32[]{:S(2)}) collective-permute-start(bf16[16,488]{0,1:T(8,128)(2,1)S(1)} %copy.68), channel_id=1, source_target_pairs={{0,64},{64,0},{4,68},{68,4},{8,72},{72,8},{12,76},{76,12},{16,80},... | collective-permute-start | bytes 46856 | tf_op jit(solution)/shard_map/ppermute | solution.py:14
  49.6 12.8 %copy-start.2 = (s32[10,1024]{1,0:T(8,128)S(1)}, s32[10,1024]{1,0:T(8,128)}, u32[]{:S(2)}) copy-start(s32[10,1024]{1,0:T(8,128)} %get-tuple-element.7) | copy-start | bytes 122884
  54.1 11.1 %collective-permute-start.11 = (bf16[16,488]{0,1:T(8,128)(2,1)S(1)}, bf16[16,488]{0,1:T(8,128)(2,1)S(1)}, u32[]{:S(2)}, u32[]{:S(2)}) collective-permute-start(bf16[16,488]{0,1:T(8,128)(2,1)S(1)} %copy.70), channel_id=1, source_target_pairs={{0,128},{128,0},{4,132},{132,4},{8,136},{136,8},{12,140},{140,12},... | collective-permute-start | bytes 46856 | tf_op jit(solution)/shard_map/ppermute | solution.py:14
  73.3 6.0 %collective-permute-start.2 = (bf16[64,488]{1,0:T(8,128)(2,1)}, bf16[64,488]{1,0:T(8,128)(2,1)S(1)}, u32[]{:S(2)}, u32[]{:S(2)}) collective-permute-start(bf16[64,488]{1,0:T(8,128)(2,1)} %gather_fusion.2), channel_id=1, source_target_pairs={{0,16},{16,0},{4,20},{20,4},{8,24},{24,8},{12,28},{28,12},{32,48},... | collective-permute-start | bytes 187400 | tf_op jit(solution)/shard_map/ppermute | solution.py:14
  80.7 5.8 %collective-permute-start.3 = (bf16[64,488]{1,0:T(8,128)(2,1)}, bf16[64,488]{1,0:T(8,128)(2,1)S(1)}, u32[]{:S(2)}, u32[]{:S(2)}) collective-permute-start(bf16[64,488]{1,0:T(8,128)(2,1)} %gather_fusion.3), channel_id=1, source_target_pairs={{0,32},{32,0},{4,36},{36,4},{8,40},{40,8},{12,44},{44,12},{16,48},... | collective-permute-start | bytes 187400 | tf_op jit(solution)/shard_map/ppermute | solution.py:14
  87.4 6.9 %collective-permute-start.4 = (bf16[64,488]{1,0:T(8,128)(2,1)S(1)}, bf16[64,488]{1,0:T(8,128)(2,1)S(1)}, u32[]{:S(2)}, u32[]{:S(2)}) collective-permute-start(bf16[64,488]{1,0:T(8,128)(2,1)S(1)} %gather_fusion.4), channel_id=1, source_target_pairs={{0,64},{64,0},{4,68},{68,4},{8,72},{72,8},{12,76},{76,12},{16,80},... | collective-permute-start | bytes 187400 | tf_op jit(solution)/shard_map/ppermute | solution.py:14
  95.8 13.9 %collective-permute-start.5 = (bf16[64,488]{1,0:T(8,128)(2,1)}, bf16[64,488]{1,0:T(8,128)(2,1)}, u32[]{:S(2)}, u32[]{:S(2)}) collective-permute-start(bf16[64,488]{1,0:T(8,128)(2,1)} %gather_fusion.5), channel_id=1, source_target_pairs={{0,128},{128,0},{4,132},{132,4},{8,136},{136,8},{12,140},{140,12},... | collective-permute-start | bytes 187400 | tf_op jit(solution)/shard_map/ppermute | solution.py:14
  155.6 21.2 %copy-start.1 = (pred[1024,10]{1,0:T(8,128)(4,1)S(1)}, pred[1024,10]{1,0:T(8,128)(4,1)}, u32[]{:S(2)}) copy-start(pred[1024,10]{1,0:T(8,128)(4,1)} %copy.52) | copy-start | bytes 30724
  155.6 36.6 %slice-start = ((s8[4997120]{0:T(1024)(128)(4,1)}), s8[802816]{0:T(1024)(128)(4,1)S(1)}, s32[]{:S(2)}) async-start(s8[4997120]{0:T(1024)(128)(4,1)} %bitcast.90), calls=%async_computation.6 | async-start | bytes 1605632
  176.8 15.4 %slice-start.1 = ((s8[4997120]{0:T(1024)(128)(4,1)}), s8[4194304]{0:T(1024)(128)(4,1)S(1)}, s32[]{:S(2)}) async-start(s8[4997120]{0:T(1024)(128)(4,1)} %bitcast.90), calls=%async_computation.7 | async-start | bytes 8388608
  176.8 15.4 %copy-start = (f32[1024,488]{0,1:T(8,128)S(1)}, f32[1024,488]{0,1:T(8,128)}, u32[]{:S(2)}) copy-start(f32[1024,488]{0,1:T(8,128)} %copy.76) | copy-start | bytes 5996548
Sparse Core Ops, SparseCore 0:
  19.0 2.2 sort.39.cloned.1.call-done
  24.1 4.3 sort.37.cloned.1.call-done
  208.5 28.8 reduce-scatter.1
  (2 shorter events, 0.0 us)
